TPU v7x, 128 devices: a whole 4x4x4 slice. The times are simulated.
128 devices in a mesh: dp: 32 (over y, z, core), tensor: 4 (over x).
Axes of the slice: x: 4, y: 4, z: 4, core: 2. Of those that a mesh axis runs over, the one named last changes fastest.
Arguments:
- tokens: bfloat16 [16384, 4096], P('dp', 'tensor'), may hold values from -6 to 6
- grad_out: bfloat16 [16384, 4096], P('dp'), may hold values from -3 to 3
- gate_pre: bfloat16 [16384, 14336], P('dp', 'tensor'), may hold values from -9 to 9
- up_value: bfloat16 [16384, 14336], P('dp', 'tensor'), may hold values from -6 to 6
- down_weight: bfloat16 [14336, 4096], P('tensor', 'dp'), may hold values from -0.09375 to 0.09375
- in_proj: bfloat16 [128, 4096], P(None, 'tensor'), may hold values from -0.09375 to 0.09375
- out_proj: bfloat16 [128, 14336], P(None, 'tensor'), may hold values from -0.046875 to 0.046875
- test_matrix: bfloat16 [16384, 128], replicated, may hold values from -0.046875 to 0.046875
Outputs:
- factor: float32 [16384, 128], P(('dp', 'tensor'))
All inputs are finite; a program needn't handle non-finite values.
Results may differ from a plain program's by a relative error of at most 0.0065.
The roundings to bfloat16 on the way count: a program that leaves them out, or rounds other values in their place, can miss the bound.
Values may be sent and summed in bfloat16 or wider, within the bound.
A program may use at most 128 MiB of HBM per device.

v0:
```python
import jax
import jax.numpy as jnp
from jax import lax
from jax.sharding import PartitionSpec as P

SEQ_LEN = 128
shift_scale = 0.1
tiny_value = 1e-06


def local(tokens, grad_out, gate_pre, up_value, down_weight, in_proj, out_proj, test_matrix):
    rows = grad_out.shape[0]
    hidden_grad = lax.dot_general(
        grad_out,
        lax.all_gather(down_weight, "dp", axis=1, tiled=True),
        (((1,), (1,)), ((), ())),
        preferred_element_type=jnp.float32,
    )
    gate_wide = gate_pre.astype(jnp.float32)
    logistic = jax.nn.sigmoid(gate_wide)
    gate_grad = (
        hidden_grad * up_value.astype(jnp.float32) * logistic * (1.0 + gate_wide * (1.0 - logistic))
    ).astype(jnp.bfloat16)
    act_part = lax.dot_general(
        tokens, in_proj, (((1,), (1,)), ((), ())), preferred_element_type=jnp.float32
    )
    out_part = lax.dot_general(
        gate_grad, out_proj, (((1,), (1,)), ((), ())), preferred_element_type=jnp.float32
    )
    act_sum, out_sum = lax.psum((act_part, out_part), "tensor")
    pdim = in_proj.shape[0]
    rank_cols = test_matrix.shape[1]
    seqs_here = rows // SEQ_LEN
    act_seq = act_sum.astype(jnp.bfloat16).reshape(seqs_here, SEQ_LEN, pdim)
    out_seq = out_sum.astype(jnp.bfloat16).reshape(seqs_here, SEQ_LEN, pdim)
    proj_grad = (
        jnp.einsum("slp,slq->spq", act_seq, out_seq, preferred_element_type=jnp.float32)
        .astype(jnp.bfloat16)
        .reshape(seqs_here, pdim * pdim)
    )
    coeff = jnp.dot(proj_grad, test_matrix, preferred_element_type=jnp.float32).astype(jnp.bfloat16)
    dp_count = lax.axis_size("dp")
    tp_count = lax.axis_size("tensor")
    tp_index = lax.axis_index("tensor")
    dp_index = lax.axis_index("dp")
    width = pdim * pdim // (dp_count * tp_count)
    picked = lax.dynamic_slice_in_dim(
        proj_grad.reshape(seqs_here, dp_count, tp_count, width), tp_index, 1, 2
    ).reshape(seqs_here, dp_count * width)
    omega_wide = test_matrix.astype(jnp.float32)
    omega_picked = lax.dynamic_slice_in_dim(
        omega_wide.reshape(dp_count, tp_count, width, rank_cols), tp_index, 1, 1
    ).reshape(dp_count * width, rank_cols)
    omega_own = lax.dynamic_slice_in_dim(omega_picked, dp_index * width, width, 0)
    sketch_part = lax.dot_general(
        picked, coeff, (((0,), (0,)), ((), ())), preferred_element_type=jnp.float32
    )
    gram = lax.dot_general(
        test_matrix, test_matrix, (((0,), (0,)), ((), ())), preferred_element_type=jnp.float32
    )
    omega_sq = jnp.trace(gram)
    summed = lax.psum(sketch_part, "dp")
    core_local = lax.dot_general(
        omega_picked, summed, (((0,), (0,)), ((), ())), precision=lax.Precision.HIGHEST
    )
    square_sum, core_sketch = lax.psum((jnp.sum(summed * summed), core_local), "tensor")
    own_rows = lax.dynamic_slice_in_dim(summed, dp_index * width, width, 0)
    shift = shift_scale * jnp.sqrt(square_sum / (omega_sq + tiny_value))
    core = core_sketch + shift * gram
    core = 0.5 * (core + core.T)
    lower = jnp.linalg.cholesky(core)
    shifted = own_rows + shift * omega_own
    factor = jax.scipy.linalg.solve_triangular(lower, shifted.T, lower=True).T
    return factor


def solution(mesh):
    in_specs = (
        P("dp", "tensor"),
        P("dp", None),
        P("dp", "tensor"),
        P("dp", "tensor"),
        P("tensor", "dp"),
        P(None, "tensor"),
        P(None, "tensor"),
        P(),
    )
    out_specs = P(("dp", "tensor"), None)
    return jax.shard_map(local, mesh=mesh, in_specs=in_specs, out_specs=out_specs, check_vma=False)
```

profile of v0, /device:TPU:0, one launch (start us, length us, event | category | flops | bytes accessed | tf_op | source)
XLA Modules:
  0.0 362.2 jit_solution(9847140538251873871)
XLA Ops:
  6.5 0.0 copy-start
  6.5 0.0 all-gather.2.cloned.1.call-start
  6.5 0.7 all-gather.2.cloned.1.call-update
  7.3 0.0 all-reduce.5.cloned.1.call-start
  7.3 0.5 copy-done
  7.8 1.4 fusion.24
  9.1 116.3 %all-gather.2.cloned.1.call-done = bf16[3584,4096]{1,0:T(8,128)(2,1)} async-done(((bf16[3584,128]{1,0:T(8,128)(2,1)}), bf16[3584,4096]{1,0:T(8,128)(2,1)}) %all-gather.2.cloned.1.call-update) | async-done | bytes 29360144 | tf_op jit(solution)/shard_map/all_gather | solution.py:15
  125.4 24.7 %fusion.25 = f32[512,128]{1,0:T(8,128)S(1)} fusion(bf16[128,3584]{1,0:T(8,128)(2,1)} %param.14, bf16[512,3584]{1,0:T(8,128)(2,1)} %param.10, bf16[512,3584]{1,0:T(8,128)(2,1)} %param.11, bf16[512,4096]{1,0:T(8,128)(2,1)} %param.9, bf16[3584,4096]{1,0:T(8,128)(2,1)} %all-gather.2.cloned.1.call-done), kind=kOutput, calls=%fused_computation.40 | convolution fusion | flops 15524167680 | bytes 42074112 | tf_op jit(solution)/shard_map/dot_general | solution.py:27
  150.1 23.1 %all-reduce.8 = (bf16[512,128]{1,0:T(8,128)(2,1)S(1)}, bf16[512,128]{1,0:T(8,128)(2,1)S(1)}) all-reduce(f32[512,128]{1,0:T(8,128)S(1)} %fusion.24, f32[512,128]{1,0:T(8,128)S(1)} %fusion.25), channel_id=1, replica_groups=mesh['dp'=32,'tensor'=4] {'tensor'}, use_global_device_ids=true, to_apply=%region_0.0 | all-reduce | flops 131072 | bytes 786432 | tf_op jit(solution)/shard_map/psum | solution.py:30
  173.2 0.2 convolution_convert_fusion
  173.4 0.2 dynamic-slice_reduce_fusion
  173.6 4.7 %fusion.6 = f32[4096,128]{0,1:T(8,128)} fusion(bf16[16384,128]{1,0:T(8,128)(2,1)} %param.15, bf16[1,4,128,128]{3,2,1,0:T(8,128)(2,1)S(1)} %bitcast.60, bf16[1,4,32,128]{3,2,1,0:T(8,128)(2,1)S(1)} %bitcast.61), kind=kOutput, calls=%fused_computation.12 | convolution fusion | flops 20972032 | bytes 6455296 | tf_op jit(solution)/shard_map/dot_general | solution.py:55
  178.3 0.0 all-reduce.5.cloned.1.call-update
  178.3 0.2 all-reduce.7.cloned.1.call-start
  178.6 5.4 %select_reduce_fusion.1 = (f32[]{:T(128)}, f32[128,128]{1,0:T(8,128)S(1)}) fusion(bf16[16384,128]{1,0:T(8,128)(2,1)} %param.15), kind=kOutput, calls=%fused_computation.29 | convolution fusion | flops 536920064 | bytes 4259844 | tf_op jit(solution)/shard_map/dot_general | solution.py:58
  183.9 0.1 copy.21
  184.0 1.3 constant_dynamic-slice_fusion
  185.3 1.0 copy.28
  186.3 0.3 reshape.38
  186.6 2.9 copy.42
  189.5 96.2 %all-reduce.5.cloned.1.call-done = f32[4096,128]{0,1:T(8,128)} async-done(((f32[4096,128]{0,1:T(8,128)}), f32[4096,128]{0,1:T(8,128)}) %all-reduce.5.cloned.1.call-update) | async-done | bytes 2097168 | tf_op jit(solution)/shard_map/psum | solution.py:62
  285.7 3.3 fusion.26
  289.0 0.0 all-reduce.7.cloned.1.call-update
  289.1 2.7 multiply_reduce_fusion
  292.4 10.9 %psum.38 = f32[]{:T(128)} all-reduce(f32[]{:T(128)} %multiply_reduce_fusion), channel_id=1, replica_groups=mesh['dp'=32,'tensor'=4] {'tensor'}, use_global_device_ids=true, to_apply=%region_4.5 | all-reduce | flops 1 | bytes 8 | tf_op jit(solution)/shard_map/psum | solution.py:66
  303.9 26.1 %all-reduce.7.cloned.1.call-done = f32[128,128]{0,1:T(8,128)} async-done(((f32[128,128]{0,1:T(8,128)}), f32[128,128]{0,1:T(8,128)}) %all-reduce.7.cloned.1.call-update) | async-done | bytes 65552 | tf_op jit(solution)/shard_map/psum | solution.py:66
  330.0 0.8 multiply_add_fusion
  330.8 0.1 copy.22
  330.9 0.1 copy.23
  331.0 11.7 %cholesky.13 = f32[128,128]{1,0:T(8,128)S(1)} custom-call(f32[128,128]{1,0:T(8,128)S(1)} %fusion.14), custom_call_target="Cholesky" | custom-call | tf_op jit(solution)/shard_map/jit(cholesky)/cholesky | solution.py:71
  342.8 0.6 compare_reduce_fusion
  343.4 0.7 fusion.11
  344.1 9.8 %custom-call.7 = f32[1,128,128]{1,2,0:T(8,128)S(1)} custom-call(f32[1,128,128]{2,1,0:T(8,128)S(1)} %fusion.11), custom_call_target="InvertDiagBlocksLowerTriangular" | custom-call | tf_op jit(solution)/shard_map/jit(_solve_triangular)/triangular_solve | solution.py:73
  353.9 1.8 fusion.12
  (3 shorter events, 0.1 us)
Async XLA Ops:
  6.5 1.2 copy-start
  6.5 118.9 %all-gather.2.cloned.1.call-start = ((), (), s32[]{:S(2)}) async-start(), calls=%async_computation | async-start | bytes 30277632 | tf_op jit(solution)/shard_map/all_gather | solution.py:15
  7.3 278.4 %all-reduce.5.cloned.1.call-start = ((), (), s32[]{:S(2)}) async-start(), calls=%async_computation.1 | async-start | bytes 4194304 | tf_op jit(solution)/shard_map/psum | solution.py:62
  178.3 151.6 %all-reduce.7.cloned.1.call-start = ((), (), s32[]{:S(2)}) async-start(), calls=%async_computation.2 | async-start | bytes 131072 | tf_op jit(solution)/shard_map/psum | solution.py:66
Sparse Core Ops, SparseCore 0:
  9.5 115.8 all-gather.1
  178.4 107.2 all-reduce.4
  289.2 40.7 all-reduce.6
where the time goes:
time: 363 us; the launch traced here: 362 us
  waiting for transfers between devices  239 us (66%)
  matrix products  41.5 us (11%)
  blocking collectives  34 us (9%)
  other arithmetic  26.7 us (7%)
  between operations  14.4 us (4%)
  local copies, waits for them, and re-layouts  6.14 us (2%)
    all_gather x1, waiting for transfers between devices, local(): lax.all_gather(down_weight, 'dp', axis=1, tiled=True)  116 us
    psum x1, waiting for transfers between devices, local(): summed = lax.psum(sketch_part, 'dp')  96.2 us
    psum x1, waiting for transfers between devices, local(): lax.psum((jnp.sum(summed * summed), core_local), 'tensor')  26.1 us
    dot_general x1, matrix products, local(): lax.dot_general(gate_grad, out_proj, (((1,), (1,)), ((), ())), preferred_...  24.7 us
    psum x1, blocking collectives, local(): act_sum, out_sum = lax.psum((act_part, out_part), 'tensor')  23.1 us
    another operation x3, other arithmetic, local(): lower = jnp.linalg.cholesky(core)  12.4 us
    psum x1, blocking collectives, local(): lax.psum((jnp.sum(summed * summed), core_local), 'tensor')  10.9 us
    another operation x2, other arithmetic, local(): factor = jax.scipy.linalg.solve_triangular(lower, shifted.T, lower=True).T  10.5 us
  transfers between devices with their start and end apart: 3, of which 3 were waited for; matrix products, arithmetic and copies ran while one was open for 4% of the time, Pallas kernels for 0%

commit v1 on v0

--- a/solution.py
+++ b/solution.py
@@ -12,7 +12,9 @@
     rows = grad_out.shape[0]
     hidden_grad = lax.dot_general(
         grad_out,
-        lax.all_gather(down_weight, "dp", axis=1, tiled=True),
+        jnp.concatenate(
+            lax.all_to_all(jnp.stack([down_weight] * lax.axis_size("dp")), "dp", 0, 0), axis=1
+        ),
         (((1,), (1,)), ((), ())),
         preferred_element_type=jnp.float32,
     )

time: 363 us -> 744 us (2.05)
  waiting for transfers between devices: 239 us -> 601 us
  local copies, waits for them, and re-layouts: 6.14 us -> 17.3 us
  starting transfers between devices: 0.26 us -> 8.95 us
    all_to_all x0 -> x1, waiting for transfers between devices: none -> 424 us  [local(): lax.all_to_all(jnp.stack([down_weight] * lax.axis_size('dp')), 'dp', 0, 0)]
    all_gather x1 -> x0, waiting for transfers between devices: 116 us -> none  [local(): lax.all_gather(down_weight, 'dp', axis=1, tiled=True)]
    psum x1, waiting for transfers between devices: 96.2 us -> 151 us  [local(): summed = lax.psum(sketch_part, 'dp')]
    another operation x0 -> x1, local copies, waits for them, and re-layouts: none -> 10 us  [local(): jnp.stack([down_weight] * lax.axis_size('dp'))]
    all_to_all x0 -> x1, starting transfers between devices: none -> 8.69 us  [local(): lax.all_to_all(jnp.stack([down_weight] * lax.axis_size('dp')), 'dp', 0, 0)]
  transfers between devices with their start and end apart: 3 -> 3, of which waited for: 3 -> 3; matrix products, arithmetic and copies ran while one was open for 4% -> 2% of each run, Pallas kernels for 0% -> 0%
where the time goes in v1:
time: 744 us
  waiting for transfers between devices  601 us (81%)
  matrix products  40.8 us (5%)
  blocking collectives  33.8 us (5%)
  other arithmetic  26.7 us (4%)
  local copies, waits for them, and re-layouts  17.3 us (2%)
  between operations  14.8 us (2%)
  starting transfers between devices  8.95 us (1%)
    all_to_all x1, waiting for transfers between devices, local(): lax.all_to_all(jnp.stack([down_weight] * lax.axis_size('dp')), 'dp', 0, 0)  424 us
    psum x1, waiting for transfers between devices, local(): summed = lax.psum(sketch_part, 'dp')  151 us
    psum x1, waiting for transfers between devices, local(): lax.psum((jnp.sum(summed * summed), core_local), 'tensor')  26.5 us
    dot_general x1, matrix products, local(): lax.dot_general(gate_grad, out_proj, (((1,), (1,)), ((), ())), preferred_...  24.9 us
    psum x1, blocking collectives, local(): act_sum, out_sum = lax.psum((act_part, out_part), 'tensor')  22.8 us
  transfers between devices with their start and end apart: 3, of which 3 were waited for; matrix products, arithmetic and copies ran while one was open for 2% of the time, Pallas kernels for 0%

profile of v1, /device:TPU:0, one launch (start us, length us, event | category | flops | bytes accessed | tf_op | source)
XLA Modules:
  0.0 743.5 jit_solution(12576143959404909178)
XLA Ops:
  6.5 0.0 copy-start
  6.5 1.5 copy.16
  8.1 10.0 %stack.2 = bf16[32,3584,128]{1,2,0:T(8,128)(2,1)} broadcast(bf16[3584,128]{0,1:T(8,128)(2,1)S(1)} %copy.16), dimensions={1,2} | broadcast | bytes 30277632 | tf_op jit(solution)/shard_map/stack | solution.py:16
  18.1 0.0 copy-start.2
  18.1 0.0 copy-start.3
  18.1 8.7 %all-to-all-start = ((bf16[32,3584,128]{1,2,0:T(8,128)(2,1)}), bf16[32,3584,128]{1,2,0:T(8,128)(2,1)}, u32[]{:S(2)}, u32[]{:S(2)}) async-start(bf16[32,3584,128]{1,2,0:T(8,128)(2,1)} %stack.2), calls=%async_computation | async-start | bytes 58720256 | tf_op jit(solution)/shard_map/all_to_all | solution.py:16
  26.8 0.0 all-reduce.5.cloned.1.call-start
  26.9 0.0 copy-done
  26.9 0.0 copy-done.2
  26.9 0.4 fusion.26
  27.3 424.1 %all-to-all-done = bf16[32,3584,128]{1,2,0:T(8,128)(2,1)} async-done(((bf16[32,3584,128]{1,2,0:T(8,128)(2,1)}), bf16[32,3584,128]{1,2,0:T(8,128)(2,1)}, u32[]{:S(2)}, u32[]{:S(2)}) %all-to-all-start) | async-done | bytes 29360160 | tf_op jit(solution)/shard_map/all_to_all | solution.py:16
  451.4 0.0 copy-done.3
  451.4 24.9 %fusion.7 = f32[512,128]{1,0:T(8,128)S(1)} fusion(bf16[128,3584]{1,0:T(8,128)(2,1)S(1)} %copy-done.3, bf16[512,3584]{1,0:T(8,128)(2,1)} %param.10, bf16[512,3584]{1,0:T(8,128)(2,1)} %param.11, bf16[512,4096]{1,0:T(8,128)(2,1)} %param.9, bf16[3584,4096]{0,1:T(8,128)(2,1)} %bitcast.2), kind=kOutput, calls=%fused_computation.13 | convolution fusion | flops 15524167680 | bytes 42074112 | tf_op jit(solution)/shard_map/dot_general | solution.py:29
  476.3 22.8 %all-reduce.8 = (bf16[512,128]{1,0:T(8,128)(2,1)S(1)}, bf16[512,128]{1,0:T(8,128)(2,1)S(1)}) all-reduce(f32[512,128]{1,0:T(8,128)S(1)} %fusion.26, f32[512,128]{1,0:T(8,128)S(1)} %fusion.7), channel_id=1, replica_groups=mesh['dp'=32,'tensor'=4] {'tensor'}, use_global_device_ids=true, to_apply=%region_0.0 | all-reduce | flops 131072 | bytes 786432 | tf_op jit(solution)/shard_map/psum | solution.py:32
  499.2 0.2 convolution_convert_fusion
  499.4 0.2 dynamic-slice_reduce_fusion
  499.6 4.7 fusion.6
  504.3 0.0 all-reduce.5.cloned.1.call-update
  504.3 0.2 all-reduce.7.cloned.1.call-start
  504.5 5.4 select_reduce_fusion.1
  509.9 0.1 copy.22
  510.0 1.3 constant_dynamic-slice_fusion
  511.3 1.0 copy.29
  512.3 0.3 reshape.48
  512.6 0.0 copy-start.1
  512.6 2.9 copy.43
  516.2 150.5 %all-reduce.5.cloned.1.call-done = f32[4096,128]{0,1:T(8,128)} async-done(((f32[4096,128]{0,1:T(8,128)}), f32[4096,128]{0,1:T(8,128)}) %all-reduce.5.cloned.1.call-update) | async-done | bytes 2097168 | tf_op jit(solution)/shard_map/psum | solution.py:64
  666.7 3.3 fusion.27
  670.0 0.0 all-reduce.7.cloned.1.call-update
  670.0 2.7 multiply_reduce_fusion
  672.8 11.0 %psum.38 = f32[]{:T(128)} all-reduce(f32[]{:T(128)} %multiply_reduce_fusion), channel_id=1, replica_groups=mesh['dp'=32,'tensor'=4] {'tensor'}, use_global_device_ids=true, to_apply=%region_4.5 | all-reduce | flops 1 | bytes 8 | tf_op jit(solution)/shard_map/psum | solution.py:68
  684.4 26.5 %all-reduce.7.cloned.1.call-done = f32[128,128]{0,1:T(8,128)} async-done(((f32[128,128]{0,1:T(8,128)}), f32[128,128]{0,1:T(8,128)}) %all-reduce.7.cloned.1.call-update) | async-done | bytes 65552 | tf_op jit(solution)/shard_map/psum | solution.py:68
  710.9 0.8 multiply_add_fusion
  711.8 0.1 copy.23
  711.9 0.1 copy.24
  712.0 11.7 %cholesky.13 = f32[128,128]{1,0:T(8,128)S(1)} custom-call(f32[128,128]{1,0:T(8,128)S(1)} %fusion.15), custom_call_target="Cholesky" | custom-call | tf_op jit(solution)/shard_map/jit(cholesky)/cholesky | solution.py:73
  723.8 0.6 compare_reduce_fusion
  724.4 0.7 fusion.12
  725.1 9.8 %custom-call.7 = f32[1,128,128]{1,2,0:T(8,128)S(1)} custom-call(f32[1,128,128]{2,1,0:T(8,128)S(1)} %fusion.12), custom_call_target="InvertDiagBlocksLowerTriangular" | custom-call | tf_op jit(solution)/shard_map/jit(_solve_triangular)/triangular_solve | solution.py:75
  734.9 1.8 fusion.13
  736.7 0.0 copy-done.1
  (3 shorter events, 0.1 us)
Async XLA Ops:
  6.5 20.3 %copy-start = (bf16[512,1024]{1,0:T(8,128)(2,1)S(1)}, bf16[512,1024]{1,0:T(8,128)(2,1)}, u32[]{:S(2)}) copy-start(bf16[512,1024]{1,0:T(8,128)(2,1)} %param.8) | copy-start | bytes 3145732
  18.1 8.8 %copy-start.2 = (bf16[128,1024]{1,0:T(8,128)(2,1)S(1)}, bf16[128,1024]{1,0:T(8,128)(2,1)}, u32[]{:S(2)}) copy-start(bf16[128,1024]{1,0:T(8,128)(2,1)} %param.13) | copy-start | bytes 786436
  18.1 433.3 %copy-start.3 = (bf16[128,3584]{1,0:T(8,128)(2,1)S(1)}, bf16[128,3584]{1,0:T(8,128)(2,1)}, u32[]{:S(2)}) copy-start(bf16[128,3584]{1,0:T(8,128)(2,1)} %param.14) | copy-start | bytes 2752516
  18.1 433.3 %all-to-all-start = ((bf16[32,3584,128]{1,2,0:T(8,128)(2,1)}), bf16[32,3584,128]{1,2,0:T(8,128)(2,1)}, u32[]{:S(2)}, u32[]{:S(2)}) async-start(bf16[32,3584,128]{1,2,0:T(8,128)(2,1)} %stack.2), calls=%async_computation | async-start | bytes 58720256 | tf_op jit(solution)/shard_map/all_to_all | solution.py:16
  26.8 639.9 %all-reduce.5.cloned.1.call-start = ((), (), s32[]{:S(2)}) async-start(), calls=%async_computation.1 | async-start | bytes 4194304 | tf_op jit(solution)/shard_map/psum | solution.py:64
  504.3 206.6 %all-reduce.7.cloned.1.call-start = ((), (), s32[]{:S(2)}) async-start(), calls=%async_computation.2 | async-start | bytes 131072 | tf_op jit(solution)/shard_map/psum | solution.py:68
  512.6 224.1 %copy-start.1 = (bf16[512,1024]{1,0:T(8,128)(2,1)S(1)}, bf16[512,1024]{1,0:T(8,128)(2,1)}, u32[]{:S(2)}) copy-start(bf16[512,1024]{1,0:T(8,128)(2,1)} %param.8) | copy-start | bytes 3145732
Sparse Core Ops, SparseCore 0:
  504.4 162.2 all-reduce.4
  670.2 40.7 all-reduce.6

commit v2 on v0

--- a/solution.py
+++ b/solution.py
@@ -59,7 +59,7 @@
         test_matrix, test_matrix, (((0,), (0,)), ((), ())), preferred_element_type=jnp.float32
     )
     omega_sq = jnp.trace(gram)
-    summed = lax.psum(sketch_part, "dp")
+    summed = jnp.sum(lax.all_gather(sketch_part, "dp"), axis=0)
     core_local = lax.dot_general(
         omega_picked, summed, (((0,), (0,)), ((), ())), precision=lax.Precision.HIGHEST
     )

time: 363 us -> 477 us (1.31)
  waiting for transfers between devices: 239 us -> 334 us
  other arithmetic: 26.7 us -> 46 us
    all_gather x0 -> x1, waiting for transfers between devices: none -> 189 us  [local(): summed = jnp.sum(lax.all_gather(sketch_part, 'dp'), axis=0)]
    psum x1 -> x0, waiting for transfers between devices: 96.2 us -> none  [local(): summed = lax.psum(sketch_part, 'dp')]
    reduce_sum x0 -> x1, other arithmetic: none -> 20.8 us  [local(): summed = jnp.sum(lax.all_gather(sketch_part, 'dp'), axis=0)]
  transfers between devices with their start and end apart: 3 -> 3, of which waited for: 3 -> 3; matrix products, arithmetic and copies ran while one was open for 4% -> 3% of each run, Pallas kernels for 0% -> 0%
where the time goes in v2:
time: 477 us
  waiting for transfers between devices  334 us (70%)
  other arithmetic  46 us (10%)
  matrix products  41.7 us (9%)
  blocking collectives  34.3 us (7%)
  between operations  14.6 us (3%)
  local copies, waits for them, and re-layouts  6.29 us (1%)
    all_gather x1, waiting for transfers between devices, local(): summed = jnp.sum(lax.all_gather(sketch_part, 'dp'), axis=0)  189 us
    all_gather x1, waiting for transfers between devices, local(): lax.all_gather(down_weight, 'dp', axis=1, tiled=True)  116 us
    psum x1, waiting for transfers between devices, local(): lax.psum((jnp.sum(summed * summed), core_local), 'tensor')  28.1 us
    dot_general x1, matrix products, local(): lax.dot_general(gate_grad, out_proj, (((1,), (1,)), ((), ())), preferred_...  24.7 us
    psum x1, blocking collectives, local(): act_sum, out_sum = lax.psum((act_part, out_part), 'tensor')  23.1 us
    reduce_sum x1, other arithmetic, local(): summed = jnp.sum(lax.all_gather(sketch_part, 'dp'), axis=0)  20.8 us
    another operation x3, other arithmetic, local(): lower = jnp.linalg.cholesky(core)  12.4 us
    psum x1, blocking collectives, local(): lax.psum((jnp.sum(summed * summed), core_local), 'tensor')  11.2 us
  transfers between devices with their start and end apart: 3, of which 3 were waited for; matrix products, arithmetic and copies ran while one was open for 3% of the time, Pallas kernels for 0%

profile of v2, /device:TPU:0, one launch (start us, length us, event | category | flops | bytes accessed | tf_op | source)
XLA Modules:
  0.0 477.0 jit_solution(5471397343523482794)
XLA Ops:
  6.5 0.0 copy-start
  6.5 0.0 all-gather.4.cloned.1.call-start
  6.5 0.7 all-gather.4.cloned.1.call-update
  7.3 0.0 all-gather.6.cloned.1.call-start
  7.3 0.5 copy-done
  7.8 1.4 fusion.23
  9.1 116.3 %all-gather.4.cloned.1.call-done = bf16[3584,4096]{1,0:T(8,128)(2,1)} async-done(((bf16[3584,128]{1,0:T(8,128)(2,1)}), bf16[3584,4096]{1,0:T(8,128)(2,1)}) %all-gather.4.cloned.1.call-update) | async-done | bytes 29360144 | tf_op jit(solution)/shard_map/all_gather | solution.py:15
  125.4 24.7 %fusion.24 = f32[512,128]{1,0:T(8,128)S(1)} fusion(bf16[128,3584]{1,0:T(8,128)(2,1)} %param.14, bf16[512,3584]{1,0:T(8,128)(2,1)} %param.10, bf16[512,3584]{1,0:T(8,128)(2,1)} %param.11, bf16[512,4096]{1,0:T(8,128)(2,1)} %param.9, bf16[3584,4096]{1,0:T(8,128)(2,1)} %all-gather.4.cloned.1.call-done), kind=kOutput, calls=%fused_computation.40 | convolution fusion | flops 15524167680 | bytes 42074112 | tf_op jit(solution)/shard_map/dot_general | solution.py:27
  150.1 23.1 %all-reduce.5 = (bf16[512,128]{1,0:T(8,128)(2,1)S(1)}, bf16[512,128]{1,0:T(8,128)(2,1)S(1)}) all-reduce(f32[512,128]{1,0:T(8,128)S(1)} %fusion.23, f32[512,128]{1,0:T(8,128)S(1)} %fusion.24), channel_id=1, replica_groups=mesh['dp'=32,'tensor'=4] {'tensor'}, use_global_device_ids=true, to_apply=%region_0.0 | all-reduce | flops 131072 | bytes 786432 | tf_op jit(solution)/shard_map/psum | solution.py:30
  173.2 0.2 convolution_convert_fusion
  173.4 0.2 dynamic-slice_reduce_fusion
  173.6 4.6 fusion.6
  178.3 0.0 all-gather.6.cloned.1.call-update
  178.3 0.2 all-reduce.4.cloned.1.call-start
  178.5 5.4 %select_reduce_fusion.1 = (f32[]{:T(128)}, f32[128,128]{1,0:T(8,128)S(1)}) fusion(bf16[16384,128]{1,0:T(8,128)(2,1)} %param.15), kind=kOutput, calls=%fused_computation.29 | convolution fusion | flops 536920064 | bytes 4259844 | tf_op jit(solution)/shard_map/dot_general | solution.py:58
  183.9 0.1 copy.27
  184.0 1.3 constant_dynamic-slice_fusion
  185.3 0.0 copy-start.1
  185.3 1.0 copy.34
  186.3 0.3 reshape.38
  186.6 3.0 copy.48
  189.5 0.0 copy-done.1
  190.2 188.8 %all-gather.6.cloned.1.call-done = f32[131072,128]{1,0:T(8,128)} async-done(((f32[4096,128]{1,0:T(8,128)}), f32[131072,128]{1,0:T(8,128)}) %all-gather.6.cloned.1.call-update) | async-done | bytes 67108880 | tf_op jit(solution)/shard_map/all_gather | solution.py:62
  379.0 20.8 %reduce_sum.28 = f32[4096,128]{1,0:T(8,128)S(1)} reduce(f32[32,4096,128]{2,1,0:T(8,128)} %bitcast.3, f32[]{:T(128)} %constant.62.clone.1), dimensions={0}, to_apply=%region_2.3 | reduce | flops 16252928 | bytes 69206016 | tf_op jit(solution)/shard_map/reduce_sum | solution.py:62
  399.8 1.2 multiply_reduce_fusion
  401.0 3.7 fusion.25
  404.6 0.0 all-reduce.4.cloned.1.call-update
  404.7 11.2 %psum.30 = f32[]{:T(128)} all-reduce(f32[]{:T(128)} %multiply_reduce_fusion), channel_id=1, replica_groups=mesh['dp'=32,'tensor'=4] {'tensor'}, use_global_device_ids=true, to_apply=%region_4.5 | all-reduce | flops 1 | bytes 8 | tf_op jit(solution)/shard_map/psum | solution.py:66
  416.6 0.1 copy.33
  416.7 28.1 %all-reduce.4.cloned.1.call-done = f32[128,128]{0,1:T(8,128)} async-done(((f32[128,128]{0,1:T(8,128)}), f32[128,128]{0,1:T(8,128)}) %all-reduce.4.cloned.1.call-update) | async-done | bytes 65552 | tf_op jit(solution)/shard_map/psum | solution.py:66
  444.8 0.8 multiply_add_fusion
  445.6 0.1 copy.28
  445.8 0.1 copy.29
  445.9 11.7 %cholesky.13 = f32[128,128]{1,0:T(8,128)S(1)} custom-call(f32[128,128]{1,0:T(8,128)S(1)} %fusion.14), custom_call_target="Cholesky" | custom-call | tf_op jit(solution)/shard_map/jit(cholesky)/cholesky | solution.py:71
  457.6 0.6 compare_reduce_fusion
  458.3 0.7 fusion.11
  458.9 9.8 %custom-call.7 = f32[1,128,128]{1,2,0:T(8,128)S(1)} custom-call(f32[1,128,128]{2,1,0:T(8,128)S(1)} %fusion.11), custom_call_target="InvertDiagBlocksLowerTriangular" | custom-call | tf_op jit(solution)/shard_map/jit(_solve_triangular)/triangular_solve | solution.py:73
  468.7 1.8 fusion.12
  (4 shorter events, 0.1 us)
Async XLA Ops:
  6.5 1.2 copy-start
  6.5 118.9 %all-gather.4.cloned.1.call-start = ((), (), s32[]{:S(2)}) async-start(), calls=%async_computation | async-start | bytes 30277632 | tf_op jit(solution)/shard_map/all_gather | solution.py:15
  7.3 371.7 %all-gather.6.cloned.1.call-start = ((), (), s32[]{:S(2)}) async-start(), calls=%async_computation.2 | async-start | bytes 69206016 | tf_op jit(solution)/shard_map/all_gather | solution.py:62
  178.3 266.5 %all-reduce.4.cloned.1.call-start = ((), (), s32[]{:S(2)}) async-start(), calls=%async_computation.1 | async-start | bytes 131072 | tf_op jit(solution)/shard_map/psum | solution.py:66
  185.3 4.2 copy-start.1
Sparse Core Ops, SparseCore 0:
  9.5 115.8 all-gather.3
  178.4 200.5 all-gather.5
  404.8 39.9 all-reduce.3
